TPU v7x, 32 devices: a whole 2x2x4 slice. The times are simulated.
32 devices in a mesh: gx: 16 (over z, y, core), gy: 2 (over x).
Axes of the slice: x: 2, y: 2, z: 4, core: 2. Of those that a mesh axis runs over, the one named last changes fastest.
Arguments:
- tangent: bfloat16 [256, 1024, 256], P(None, 'gx', 'gy'), may hold values from -6 to 6
- courant_x: float32 [1024, 256], P('gx', 'gy'), may hold values from -0.5 to 0.5
- courant_y: float32 [1024, 256], P('gx', 'gy'), may hold values from -0.5 to 0.5
- growth: float32 [1024, 256], P('gx', 'gy'), may hold values from -0.15 to 0.15
Outputs:
- basis: bfloat16 [256, 1024, 256], P(None, 'gx', 'gy')
- factor: float32 [256, 256], replicated
- exponents: float32 [256], replicated
All inputs are finite; a program needn't handle non-finite values.
Results may differ from a plain program's by a relative error of at most 0.001.
The roundings to bfloat16 on the way count: a program that leaves them out, or rounds other values in their place, can miss the bound.
Values may be sent and summed in bfloat16 or wider, within the bound.
No kernel may reach another device: no remote copies, remote signals or barrier semaphores. Data moves between devices by JAX's collectives and lax.ppermute only.
A program may use at most 128 MiB of HBM per device.

v0:
```python
import jax
import jax.numpy as jnp
from jax import lax
from jax.sharding import PartitionSpec as P

SUBSTEPS = 4


def extended(block, sides, width):
    for axis, dim in sides:
        count = lax.axis_size(axis)
        forward = [(i, i + 1) for i in range(count - 1)]
        forward.append((count - 1, 0))
        backward = [(target, source) for source, target in forward]
        low = lax.ppermute(
            lax.slice_in_dim(block, block.shape[dim] - width, None, axis=dim), axis, forward
        )
        high = lax.ppermute(lax.slice_in_dim(block, 0, width, axis=dim), axis, backward)
        block = jnp.concatenate([low, block, high], axis=dim)
    return block


def advance(padded, courant_x, courant_y, growth):
    centre = padded[:, 1:-1, 1:-1]
    north = padded[:, 2:, 1:-1]
    south = padded[:, :-2, 1:-1]
    east = padded[:, 1:-1, 2:]
    west = padded[:, 1:-1, :-2]
    return (
        centre
        + 0.2 * (north + south + east + west - 4.0 * centre)
        - courant_x * (north - south)
        - courant_y * (east - west)
        + growth * centre
    )


def inner_products(left, right):
    return lax.dot_general(
        left, right, (((1,), (1,)), ((), ())), preferred_element_type=jnp.float32
    )


def per_device(tangent, courant_x, courant_y, growth):
    fields, rows, cols = tangent.shape
    steps = SUBSTEPS
    state = tangent.astype(jnp.float32)
    for step in range(steps):
        padded = extended(state, (("gx", 1), ("gy", 2)), 1)
        state = advance(padded, courant_x, courant_y, growth)
    evolved = state.astype(jnp.bfloat16).reshape(fields, rows * cols)
    total = jnp.float32(rows * lax.axis_size("gx") * cols * lax.axis_size("gy"))
    gram = lax.psum(inner_products(evolved, evolved), ("gx", "gy"))
    gram = gram / total
    lower = jnp.linalg.cholesky(gram)
    inverse = lax.linalg.triangular_solve(
        lower, jnp.eye(fields, dtype=jnp.float32), left_side=True, lower=True
    ).astype(jnp.bfloat16)
    basis = jnp.dot(inverse, evolved, preferred_element_type=jnp.float32)
    exponents = jnp.log(jnp.diagonal(lower))
    return (basis.astype(jnp.bfloat16).reshape(fields, rows, cols), lower.T, exponents)


def solution(mesh):
    placed = (P(None, "gx", "gy"), P("gx", "gy"), P("gx", "gy"), P("gx", "gy"))
    return jax.shard_map(
        per_device,
        mesh=mesh,
        in_specs=placed,
        out_specs=(P(None, "gx", "gy"), P(), P()),
        check_vma=False,
    )
```

profile of v0, /device:TPU:0, one launch (start us, length us, event | category | flops | bytes accessed | tf_op | source)
XLA Modules:
  0.0 358.3 jit_solution(11706130082598331027)
XLA Ops:
  7.2 6.8 %copy.53 = bf16[256,64,128]{0,2,1:T(8,128)(2,1)} copy(bf16[256,64,128]{2,1,0:T(8,128)(2,1)} %param.4) | data formatting | bytes 8388608 | tf_op args[0]
  15.0 5.5 %collective-permute-start = (f32[256,1,128]{2,0,1:T(8,128)S(1)}, f32[256,1,128]{2,0,1:T(8,128)S(1)}, u32[]{:S(2)}, u32[]{:S(2)}) collective-permute-start(f32[256,1,128]{2,0,1:T(8,128)S(1)} %copy.54), channel_id=1, source_target_pairs={{2,0},{4,2},{6,4},{8,6},{10,8},{12,10},{14,12},{16,14},{18,16},{20... | collective-permute-start | bytes 393224 | tf_op jit(solution)/shard_map/ppermute | solution.py:18
  20.7 6.6 %convert_element_type.11 = f32[256,64,128]{0,2,1:T(8,128)} convert(bf16[256,64,128]{0,2,1:T(8,128)(2,1)} %copy.53) | non-fusion elementwise | flops 2097152 | bytes 12582912 | tf_op jit(solution)/shard_map/convert_element_type | solution.py:47
  35.4 14.9 %multiply_add_fusion.2 = f32[256,64,128]{0,2,1:T(8,128)S(1)} fusion(f32[256,64,128]{0,2,1:T(8,128)S(1)} %copy-done.6, f32[256,1,128]{0,2,1:T(8,128)S(1)} %copy.55, f32[256,1,128]{0,2,1:T(8,128)S(1)} %copy.57, f32[256,66,1]{0,2,1:T(1,128)S(1)} %copy.63, f32[256,66,1]{0,2,1:T(1,128)S(1)} %copy.61, f32[64,128]{1,0:T(8,128)S(1)} %copy-done.8, ...), kind=kLoop, calls=%fused_computation.39 | loop fusion | flops 48234496 | bytes 17272832 | tf_op jit(solution)/shard_map/add | solution.py:30
  50.4 3.3 copy-done.2
  53.7 2.7 collective-permute-start.4
  56.6 2.4 collective-permute-done.4
  59.1 4.6 %collective-permute-done.5 = f32[256,1,128]{2,0,1:T(8,128)S(1)} collective-permute-done((f32[256,1,128]{2,0,1:T(8,128)S(1)}, f32[256,1,128]{2,0,1:T(8,128)S(1)}, u32[]{:S(2)}, u32[]{:S(2)}) %collective-permute-start.5) | collective-permute-done | bytes 131104 | tf_op jit(solution)/shard_map/ppermute | solution.py:15
  70.8 14.9 %multiply_add_fusion.1 = f32[256,64,128]{0,2,1:T(8,128)S(1)} fusion(f32[256,64,128]{0,2,1:T(8,128)S(1)} %copy-done.3, f32[256,1,128]{0,2,1:T(8,128)S(1)} %copy.65, f32[256,1,128]{0,2,1:T(8,128)S(1)} %copy.67, f32[256,66,1]{0,2,1:T(1,128)S(1)} %copy.73, f32[256,66,1]{0,2,1:T(1,128)S(1)} %copy.71, f32[64,128]{1,0:T(8,128)S(1)} %copy-done.8, ...), kind=kLoop, calls=%fused_computation.38 | loop fusion | flops 48234496 | bytes 17272832 | tf_op jit(solution)/shard_map/add | solution.py:30
  85.8 3.3 copy-done.4
  91.8 4.6 %collective-permute-done.9 = f32[256,1,128]{2,0,1:T(8,128)S(1)} collective-permute-done((f32[256,1,128]{2,0,1:T(8,128)S(1)}, f32[256,1,128]{2,0,1:T(8,128)S(1)}, u32[]{:S(2)}, u32[]{:S(2)}) %collective-permute-start.9) | collective-permute-done | bytes 131104 | tf_op jit(solution)/shard_map/ppermute | solution.py:15
  103.5 14.9 %multiply_add_fusion = f32[256,64,128]{0,2,1:T(8,128)S(1)} fusion(f32[256,64,128]{0,2,1:T(8,128)S(1)} %copy-done.5, f32[256,1,128]{0,2,1:T(8,128)S(1)} %copy.75, f32[256,1,128]{0,2,1:T(8,128)S(1)} %copy.77, f32[256,66,1]{0,2,1:T(1,128)S(1)} %copy.83, f32[256,66,1]{0,2,1:T(1,128)S(1)} %copy.81, f32[64,128]{1,0:T(8,128)S(1)} %copy-done.8, ...), kind=kLoop, calls=%fused_computation.37 | loop fusion | flops 48234496 | bytes 17272832 | tf_op jit(solution)/shard_map/add | solution.py:30
  118.4 3.3 copy-done
  124.5 4.6 %collective-permute-done.13 = f32[256,1,128]{2,0,1:T(8,128)S(1)} collective-permute-done((f32[256,1,128]{2,0,1:T(8,128)S(1)}, f32[256,1,128]{2,0,1:T(8,128)S(1)}, u32[]{:S(2)}, u32[]{:S(2)}) %collective-permute-start.13) | collective-permute-done | bytes 131104 | tf_op jit(solution)/shard_map/ppermute | solution.py:15
  136.3 15.4 %add_convert_fusion = bf16[256,64,128]{0,2,1:T(8,128)(2,1)S(1)} fusion(f32[256,64,128]{0,2,1:T(8,128)S(1)} %copy-done.1, f32[256,1,128]{0,2,1:T(8,128)S(1)} %copy.85, f32[256,1,128]{0,2,1:T(8,128)S(1)} %copy.87, f32[256,66,1]{0,2,1:T(1,128)S(1)} %copy.93, f32[256,66,1]{0,2,1:T(1,128)S(1)} %copy.91, f32[64,128]{1,0:T(8,128)S(1)} %copy-done.8, ...), kind=kLoop, calls=%fused_computation.36 | loop fusion | flops 50331648 | bytes 13078528 | tf_op jit(solution)/shard_map/convert_element_type | solution.py:51
  153.7 2.5 convolution_bitcast_fusion
  156.3 121.8 %all-reduce.3.cloned.1.call-done = f32[256,256]{0,1:T(8,128)} async-done(((f32[256,256]{0,1:T(8,128)}), f32[256,256]{0,1:T(8,128)}) %all-reduce.3.cloned.1.call-update) | async-done | bytes 262160 | tf_op jit(solution)/shard_map/psum | solution.py:53
  280.1 11.7 %cholesky.50 = f32[128,128]{1,0:T(8,128)S(1)} custom-call(f32[128,128]{1,0:T(8,128)S(1)} %cholesky.118), custom_call_target="Cholesky" | custom-call | tf_op jit(solution)/shard_map/jit(cholesky)/cholesky | solution.py:55
  291.9 9.8 %custom-call.14 = f32[1,128,128]{1,2,0:T(8,128)S(1)} custom-call(f32[1,128,128]{2,1,0:T(8,128)S(1)} %get-tuple-element.54), custom_call_target="InvertDiagBlocksLowerTriangular" | custom-call | tf_op jit(solution)/shard_map/jit(cholesky)/cholesky | solution.py:55
  302.2 11.7 %cholesky.105 = f32[128,128]{1,0:T(8,128)S(1)} custom-call(f32[128,128]{1,0:T(8,128)S(1)} %convolution_subtract_fusion.1), custom_call_target="Cholesky" | custom-call | tf_op jit(solution)/shard_map/jit(cholesky)/cholesky | solution.py:55
  316.2 4.3 %while.1 = (s32[]{:T(128)}, f32[256,256]{1,0:T(8,128)S(1)}, s32[2,2]{1,0:T(2,128)S(1)}, f32[2,128,128]{2,1,0:T(8,128)S(1)}, s32[]{:T(128)}) while((s32[]{:T(128)}, f32[256,256]{1,0:T(8,128)S(1)}, s32[2,2]{1,0:T(2,128)S(1)}, f32[2,128,128]{2,1,0:T(8,128)S(1)}, s32[]{:T(128)}) %tuple.41), condition=%wide.while_cond, body=%wide.while_body.sunk | while | flops 2 | bytes 131181 | solution.py:56
  320.4 19.7 %custom-call.15 = f32[2,128,128]{1,2,0:T(8,128)S(1)} custom-call(f32[2,128,128]{2,1,0:T(8,128)S(1)} %get-tuple-element.10), custom_call_target="InvertDiagBlocksLowerTriangular" | custom-call | tf_op jit(solution)/shard_map/triangular_solve | solution.py:56
  341.0 3.5 fusion
  344.5 3.2 copy.103
  (115 shorter events, 50.5 us)
Async XLA Ops:
  7.2 270.9 %all-reduce.3.cloned.1.call-start = ((), (), s32[]{:S(2)}) async-start(), calls=%async_computation | async-start | bytes 524288 | tf_op jit(solution)/shard_map/psum | solution.py:53
  15.0 12.3 %collective-permute-start = (f32[256,1,128]{2,0,1:T(8,128)S(1)}, f32[256,1,128]{2,0,1:T(8,128)S(1)}, u32[]{:S(2)}, u32[]{:S(2)}) collective-permute-start(f32[256,1,128]{2,0,1:T(8,128)S(1)} %copy.54), channel_id=1, source_target_pairs={{2,0},{4,2},{6,4},{8,6},{10,8},{12,10},{14,12},{16,14},{18,16},{20... | collective-permute-start | bytes 393224 | tf_op jit(solution)/shard_map/ppermute | solution.py:18
  20.6 14.8 %copy-start.8 = (f32[64,128]{1,0:T(8,128)S(1)}, f32[64,128]{1,0:T(8,128)}, u32[]{:S(2)}) copy-start(f32[64,128]{1,0:T(8,128)} %param.7) | copy-start | bytes 98308
  20.6 14.8 %copy-start.9 = (f32[64,128]{1,0:T(8,128)S(1)}, f32[64,128]{1,0:T(8,128)}, u32[]{:S(2)}) copy-start(f32[64,128]{1,0:T(8,128)} %param.6) | copy-start | bytes 98308
  20.7 14.7 %copy-start.10 = (f32[64,128]{1,0:T(8,128)S(1)}, f32[64,128]{1,0:T(8,128)}, u32[]{:S(2)}) copy-start(f32[64,128]{1,0:T(8,128)} %param.5) | copy-start | bytes 98308
  20.7 7.1 %collective-permute-start.1 = (f32[256,1,128]{2,0,1:T(8,128)S(1)}, f32[256,1,128]{2,0,1:T(8,128)S(1)}, u32[]{:S(2)}, u32[]{:S(2)}) collective-permute-start(f32[256,1,128]{2,0,1:T(8,128)S(1)} %copy.56), channel_id=1, source_target_pairs={{0,2},{2,4},{4,6},{6,8},{8,10},{10,12},{12,14},{14,16},{16,18},{18... | collective-permute-start | bytes 393224 | tf_op jit(solution)/shard_map/ppermute | solution.py:15
  27.9 7.5 %copy-start.6 = (f32[256,64,128]{0,2,1:T(8,128)S(1)}, f32[256,64,128]{0,2,1:T(8,128)}, u32[]{:S(2)}) copy-start(f32[256,64,128]{0,2,1:T(8,128)} %convert_element_type.11) | copy-start | bytes 25165828
  29.4 4.4 %collective-permute-start.2 = (f32[256,66,1]{0,1,2:T(8,128)S(1)}, f32[256,66,1]{0,1,2:T(8,128)S(1)}, u32[]{:S(2)}, u32[]{:S(2)}) collective-permute-start(f32[256,66,1]{0,1,2:T(8,128)S(1)} %copy.60), channel_id=1, source_target_pairs={{1,0},{0,1},{3,2},{2,3},{5,4},{4,5},{7,6},{6,7},{9,8},{8,9},{11,10... | collective-permute-start | bytes 202760 | tf_op jit(solution)/shard_map/ppermute | solution.py:18
  30.9 4.4 %collective-permute-start.3 = (f32[256,66,1]{0,1,2:T(8,128)S(1)}, f32[256,66,1]{0,1,2:T(8,128)S(1)}, u32[]{:S(2)}, u32[]{:S(2)}) collective-permute-start(f32[256,66,1]{0,1,2:T(8,128)S(1)} %copy.62), channel_id=1, source_target_pairs={{0,1},{1,0},{2,3},{3,2},{4,5},{5,4},{6,7},{7,6},{8,9},{9,8},{10,11... | collective-permute-start | bytes 202760 | tf_op jit(solution)/shard_map/ppermute | solution.py:15
  53.7 5.2 %collective-permute-start.4 = (f32[256,1,128]{2,0,1:T(8,128)S(1)}, f32[256,1,128]{2,0,1:T(8,128)S(1)}, u32[]{:S(2)}, u32[]{:S(2)}) collective-permute-start(f32[256,1,128]{2,0,1:T(8,128)S(1)} %copy.64), channel_id=1, source_target_pairs={{2,0},{4,2},{6,4},{8,6},{10,8},{12,10},{14,12},{16,14},{18,16},{20... | collective-permute-start | bytes 393224 | tf_op jit(solution)/shard_map/ppermute | solution.py:18
  56.5 7.1 %collective-permute-start.5 = (f32[256,1,128]{2,0,1:T(8,128)S(1)}, f32[256,1,128]{2,0,1:T(8,128)S(1)}, u32[]{:S(2)}, u32[]{:S(2)}) collective-permute-start(f32[256,1,128]{2,0,1:T(8,128)S(1)} %copy.66), channel_id=1, source_target_pairs={{0,2},{2,4},{4,6},{6,8},{8,10},{10,12},{12,14},{14,16},{16,18},{18... | collective-permute-start | bytes 393224 | tf_op jit(solution)/shard_map/ppermute | solution.py:15
  63.8 7.0 %copy-start.3 = (f32[256,64,128]{0,2,1:T(8,128)S(1)}, f32[256,64,128]{0,2,1:T(8,128)}, u32[]{:S(2)}) copy-start(f32[256,64,128]{0,2,1:T(8,128)} %copy-done.2) | copy-start | bytes 25165828
  65.2 4.4 %collective-permute-start.6 = (f32[256,66,1]{0,1,2:T(8,128)S(1)}, f32[256,66,1]{0,1,2:T(8,128)S(1)}, u32[]{:S(2)}, u32[]{:S(2)}) collective-permute-start(f32[256,66,1]{0,1,2:T(8,128)S(1)} %copy.70), channel_id=1, source_target_pairs={{1,0},{0,1},{3,2},{2,3},{5,4},{4,5},{7,6},{6,7},{9,8},{8,9},{11,10... | collective-permute-start | bytes 202760 | tf_op jit(solution)/shard_map/ppermute | solution.py:18
  66.4 4.4 %collective-permute-start.7 = (f32[256,66,1]{0,1,2:T(8,128)S(1)}, f32[256,66,1]{0,1,2:T(8,128)S(1)}, u32[]{:S(2)}, u32[]{:S(2)}) collective-permute-start(f32[256,66,1]{0,1,2:T(8,128)S(1)} %copy.72), channel_id=1, source_target_pairs={{0,1},{1,0},{2,3},{3,2},{4,5},{5,4},{6,7},{7,6},{8,9},{9,8},{10,11... | collective-permute-start | bytes 202760 | tf_op jit(solution)/shard_map/ppermute | solution.py:15
  89.1 2.6 collective-permute-start.8
  89.3 7.1 %collective-permute-start.9 = (f32[256,1,128]{2,0,1:T(8,128)S(1)}, f32[256,1,128]{2,0,1:T(8,128)S(1)}, u32[]{:S(2)}, u32[]{:S(2)}) collective-permute-start(f32[256,1,128]{2,0,1:T(8,128)S(1)} %copy.76), channel_id=1, source_target_pairs={{0,2},{2,4},{4,6},{6,8},{8,10},{10,12},{12,14},{14,16},{16,18},{18... | collective-permute-start | bytes 393224 | tf_op jit(solution)/shard_map/ppermute | solution.py:15
  96.5 6.9 %copy-start.5 = (f32[256,64,128]{0,2,1:T(8,128)S(1)}, f32[256,64,128]{0,2,1:T(8,128)}, u32[]{:S(2)}) copy-start(f32[256,64,128]{0,2,1:T(8,128)} %copy-done.4) | copy-start | bytes 25165828
  98.0 4.4 %collective-permute-start.10 = (f32[256,66,1]{0,1,2:T(8,128)S(1)}, f32[256,66,1]{0,1,2:T(8,128)S(1)}, u32[]{:S(2)}, u32[]{:S(2)}) collective-permute-start(f32[256,66,1]{0,1,2:T(8,128)S(1)} %copy.80), channel_id=1, source_target_pairs={{1,0},{0,1},{3,2},{2,3},{5,4},{4,5},{7,6},{6,7},{9,8},{8,9},{11,10... | collective-permute-start | bytes 202760 | tf_op jit(solution)/shard_map/ppermute | solution.py:18
  99.1 4.4 %collective-permute-start.11 = (f32[256,66,1]{0,1,2:T(8,128)S(1)}, f32[256,66,1]{0,1,2:T(8,128)S(1)}, u32[]{:S(2)}, u32[]{:S(2)}) collective-permute-start(f32[256,66,1]{0,1,2:T(8,128)S(1)} %copy.82), channel_id=1, source_target_pairs={{0,1},{1,0},{2,3},{3,2},{4,5},{5,4},{6,7},{7,6},{8,9},{9,8},{10,11... | collective-permute-start | bytes 202760 | tf_op jit(solution)/shard_map/ppermute | solution.py:15
  121.8 2.6 collective-permute-start.12
  122.0 7.1 %collective-permute-start.13 = (f32[256,1,128]{2,0,1:T(8,128)S(1)}, f32[256,1,128]{2,0,1:T(8,128)S(1)}, u32[]{:S(2)}, u32[]{:S(2)}) collective-permute-start(f32[256,1,128]{2,0,1:T(8,128)S(1)} %copy.86), channel_id=1, source_target_pairs={{0,2},{2,4},{4,6},{6,8},{8,10},{10,12},{12,14},{14,16},{16,18},{18... | collective-permute-start | bytes 393224 | tf_op jit(solution)/shard_map/ppermute | solution.py:15
  129.2 7.0 %copy-start.1 = (f32[256,64,128]{0,2,1:T(8,128)S(1)}, f32[256,64,128]{0,2,1:T(8,128)}, u32[]{:S(2)}) copy-start(f32[256,64,128]{0,2,1:T(8,128)} %copy-done) | copy-start | bytes 25165828
  130.7 4.4 %collective-permute-start.14 = (f32[256,66,1]{0,1,2:T(8,128)S(1)}, f32[256,66,1]{0,1,2:T(8,128)S(1)}, u32[]{:S(2)}, u32[]{:S(2)}) collective-permute-start(f32[256,66,1]{0,1,2:T(8,128)S(1)} %copy.90), channel_id=1, source_target_pairs={{1,0},{0,1},{3,2},{2,3},{5,4},{4,5},{7,6},{6,7},{9,8},{8,9},{11,10... | collective-permute-start | bytes 202760 | tf_op jit(solution)/shard_map/ppermute | solution.py:18
  131.8 4.4 %collective-permute-start.15 = (f32[256,66,1]{0,1,2:T(8,128)S(1)}, f32[256,66,1]{0,1,2:T(8,128)S(1)}, u32[]{:S(2)}, u32[]{:S(2)}) collective-permute-start(f32[256,66,1]{0,1,2:T(8,128)S(1)} %copy.92), channel_id=1, source_target_pairs={{0,1},{1,0},{2,3},{3,2},{4,5},{5,4},{6,7},{7,6},{8,9},{9,8},{10,11... | collective-permute-start | bytes 202760 | tf_op jit(solution)/shard_map/ppermute | solution.py:15
  (4 other events, 11.8 us)
Sparse Core Ops, SparseCore 0:
  156.3 121.6 all-reduce.2
where the time goes:
time: 359 us; the launch traced here: 358 us
  waiting for transfers between devices  156 us (43%)
  other arithmetic  128 us (36%)
  local copies, waits for them, and re-layouts  32.9 us (9%)
  starting transfers between devices  17.9 us (5%)
  between operations  15.9 us (4%)
  matrix products  7.3 us (2%)
    psum x1, waiting for transfers between devices, per_device(): gram = lax.psum(inner_products(evolved, evolved), ('gx', 'gy'))  122 us
    add x3, other arithmetic, advance(): centre + 0.2 * (north + south + east + west - 4.0 * centre)  44.8 us
    another operation x6, other arithmetic, per_device(): lower = jnp.linalg.cholesky(gram)  34 us
    unnamed x25, local copies, waits for them, and re-layouts  22.7 us
    another operation x3, other arithmetic, per_device(): lax.linalg.triangular_solve(lower, jnp.eye(fields, dtype=jnp.float32), le...  19.7 us
    ppermute x8, waiting for transfers between devices, extended(): lax.ppermute(lax.slice_in_dim(block, block.shape[dim] - width, None, axis...  18.5 us
    convert_element_type x1, other arithmetic, per_device(): evolved = state.astype(jnp.bfloat16).reshape(fields, rows * cols)  15.4 us
    ppermute x8, waiting for transfers between devices, extended(): lax.ppermute(lax.slice_in_dim(block, 0, width, axis=dim), axis, backward)  15.4 us
  transfers between devices with their start and end apart: 17, of which 16 were waited for; matrix products, arithmetic and copies ran while one was open for 2% of the time, Pallas kernels for 0%

commit v1 on v0

--- a/solution.py
+++ b/solution.py
@@ -50,7 +50,7 @@
         state = advance(padded, courant_x, courant_y, growth)
     evolved = state.astype(jnp.bfloat16).reshape(fields, rows * cols)
     total = jnp.float32(rows * lax.axis_size("gx") * cols * lax.axis_size("gy"))
-    gram = lax.psum(inner_products(evolved, evolved), ("gx", "gy"))
+    gram = jnp.sum(lax.all_gather(inner_products(evolved, evolved), ("gx", "gy")), axis=0)
     gram = gram / total
     lower = jnp.linalg.cholesky(gram)
     inverse = lax.linalg.triangular_solve(

time: 359 us -> 313 us (0.87)
  waiting for transfers between devices: 156 us -> 108 us
    psum x1 -> x0, waiting for transfers between devices: 122 us -> none  [per_device(): gram = lax.psum(inner_products(evolved, evolved), ('gx', 'gy'))]
    all_gather x0 -> x1, waiting for transfers between devices: none -> 74.1 us  [per_device(): lax.all_gather(inner_products(evolved, evolved), ('gx', 'gy'))]
    reduce_sum x0 -> x1, other arithmetic: none -> 3.94 us  [per_device(): jnp.sum(lax.all_gather(inner_products(evolved, evolved), ('gx', 'gy')), a...]
where the time goes in v1:
time: 313 us; the launch traced here: 312 us
  other arithmetic  130 us (42%)
  waiting for transfers between devices  108 us (35%)
  local copies, waits for them, and re-layouts  32.9 us (11%)
  starting transfers between devices  17.9 us (6%)
  between operations  16.2 us (5%)
  matrix products  6.77 us (2%)
    all_gather x1, waiting for transfers between devices, per_device(): lax.all_gather(inner_products(evolved, evolved), ('gx', 'gy'))  74.1 us
    add x3, other arithmetic, advance(): centre + 0.2 * (north + south + east + west - 4.0 * centre)  44.8 us
    another operation x6, other arithmetic, per_device(): lower = jnp.linalg.cholesky(gram)  34 us
    unnamed x25, local copies, waits for them, and re-layouts  22.7 us
    another operation x3, other arithmetic, per_device(): lax.linalg.triangular_solve(lower, jnp.eye(fields, dtype=jnp.float32), le...  19.7 us
    ppermute x8, waiting for transfers between devices, extended(): lax.ppermute(lax.slice_in_dim(block, block.shape[dim] - width, None, axis...  18.5 us
    convert_element_type x1, other arithmetic, per_device(): evolved = state.astype(jnp.bfloat16).reshape(fields, rows * cols)  15.4 us
    ppermute x8, waiting for transfers between devices, extended(): lax.ppermute(lax.slice_in_dim(block, 0, width, axis=dim), axis, backward)  15.4 us
  transfers between devices with their start and end apart: 17, of which 16 were waited for; matrix products, arithmetic and copies ran while one was open for 2% of the time, Pallas kernels for 0%

profile of v1, /device:TPU:0, one launch (start us, length us, event | category | flops | bytes accessed | tf_op | source)
XLA Modules:
  0.0 312.2 jit_solution(4033694122461179209)
XLA Ops:
  7.2 6.8 %copy.50 = bf16[256,64,128]{0,2,1:T(8,128)(2,1)} copy(bf16[256,64,128]{2,1,0:T(8,128)(2,1)} %param.4) | data formatting | bytes 8388608 | tf_op args[0]
  15.0 5.5 %collective-permute-start = (f32[256,1,128]{2,0,1:T(8,128)S(1)}, f32[256,1,128]{2,0,1:T(8,128)S(1)}, u32[]{:S(2)}, u32[]{:S(2)}) collective-permute-start(f32[256,1,128]{2,0,1:T(8,128)S(1)} %copy.51), channel_id=1, source_target_pairs={{2,0},{4,2},{6,4},{8,6},{10,8},{12,10},{14,12},{16,14},{18,16},{20... | collective-permute-start | bytes 393224 | tf_op jit(solution)/shard_map/ppermute | solution.py:18
  20.7 6.6 %convert_element_type.11 = f32[256,64,128]{0,2,1:T(8,128)} convert(bf16[256,64,128]{0,2,1:T(8,128)(2,1)} %copy.50) | non-fusion elementwise | flops 2097152 | bytes 12582912 | tf_op jit(solution)/shard_map/convert_element_type | solution.py:47
  35.4 14.9 %multiply_add_fusion.2 = f32[256,64,128]{0,2,1:T(8,128)S(1)} fusion(f32[256,64,128]{0,2,1:T(8,128)S(1)} %copy-done.7, f32[256,1,128]{0,2,1:T(8,128)S(1)} %copy.52, f32[256,1,128]{0,2,1:T(8,128)S(1)} %copy.54, f32[256,66,1]{0,2,1:T(1,128)S(1)} %copy.60, f32[256,66,1]{0,2,1:T(1,128)S(1)} %copy.58, f32[64,128]{1,0:T(8,128)S(1)} %copy-done.8, ...), kind=kLoop, calls=%fused_computation.39 | loop fusion | flops 48234496 | bytes 17272832 | tf_op jit(solution)/shard_map/add | solution.py:30
  50.4 3.3 %copy-done.1 = f32[256,64,128]{0,2,1:T(8,128)} copy-done((f32[256,64,128]{0,2,1:T(8,128)}, f32[256,64,128]{0,2,1:T(8,128)S(1)}, u32[]{:S(2)}) %copy-start.1) | copy-done | bytes 8388632
  53.7 2.7 collective-permute-start.4
  56.6 2.4 collective-permute-done.4
  59.1 4.6 %collective-permute-done.5 = f32[256,1,128]{2,0,1:T(8,128)S(1)} collective-permute-done((f32[256,1,128]{2,0,1:T(8,128)S(1)}, f32[256,1,128]{2,0,1:T(8,128)S(1)}, u32[]{:S(2)}, u32[]{:S(2)}) %collective-permute-start.5) | collective-permute-done | bytes 131104 | tf_op jit(solution)/shard_map/ppermute | solution.py:15
  70.8 14.9 %multiply_add_fusion.1 = f32[256,64,128]{0,2,1:T(8,128)S(1)} fusion(f32[256,64,128]{0,2,1:T(8,128)S(1)} %copy-done.2, f32[256,1,128]{0,2,1:T(8,128)S(1)} %copy.62, f32[256,1,128]{0,2,1:T(8,128)S(1)} %copy.64, f32[256,66,1]{0,2,1:T(1,128)S(1)} %copy.70, f32[256,66,1]{0,2,1:T(1,128)S(1)} %copy.68, f32[64,128]{1,0:T(8,128)S(1)} %copy-done.8, ...), kind=kLoop, calls=%fused_computation.38 | loop fusion | flops 48234496 | bytes 17272832 | tf_op jit(solution)/shard_map/add | solution.py:30
  85.8 3.3 %copy-done.3 = f32[256,64,128]{0,2,1:T(8,128)} copy-done((f32[256,64,128]{0,2,1:T(8,128)}, f32[256,64,128]{0,2,1:T(8,128)S(1)}, u32[]{:S(2)}) %copy-start.3) | copy-done | bytes 8388632
  91.8 4.6 %collective-permute-done.9 = f32[256,1,128]{2,0,1:T(8,128)S(1)} collective-permute-done((f32[256,1,128]{2,0,1:T(8,128)S(1)}, f32[256,1,128]{2,0,1:T(8,128)S(1)}, u32[]{:S(2)}, u32[]{:S(2)}) %collective-permute-start.9) | collective-permute-done | bytes 131104 | tf_op jit(solution)/shard_map/ppermute | solution.py:15
  103.5 14.9 %multiply_add_fusion = f32[256,64,128]{0,2,1:T(8,128)S(1)} fusion(f32[256,64,128]{0,2,1:T(8,128)S(1)} %copy-done.4, f32[256,1,128]{0,2,1:T(8,128)S(1)} %copy.72, f32[256,1,128]{0,2,1:T(8,128)S(1)} %copy.74, f32[256,66,1]{0,2,1:T(1,128)S(1)} %copy.80, f32[256,66,1]{0,2,1:T(1,128)S(1)} %copy.78, f32[64,128]{1,0:T(8,128)S(1)} %copy-done.8, ...), kind=kLoop, calls=%fused_computation.37 | loop fusion | flops 48234496 | bytes 17272832 | tf_op jit(solution)/shard_map/add | solution.py:30
  118.5 3.3 %copy-done.5 = f32[256,64,128]{0,2,1:T(8,128)} copy-done((f32[256,64,128]{0,2,1:T(8,128)}, f32[256,64,128]{0,2,1:T(8,128)S(1)}, u32[]{:S(2)}) %copy-start.5) | copy-done | bytes 8388632
  124.5 4.6 %collective-permute-done.13 = f32[256,1,128]{2,0,1:T(8,128)S(1)} collective-permute-done((f32[256,1,128]{2,0,1:T(8,128)S(1)}, f32[256,1,128]{2,0,1:T(8,128)S(1)}, u32[]{:S(2)}, u32[]{:S(2)}) %collective-permute-start.13) | collective-permute-done | bytes 131104 | tf_op jit(solution)/shard_map/ppermute | solution.py:15
  136.3 15.4 %add_convert_fusion = bf16[256,64,128]{0,2,1:T(8,128)(2,1)S(1)} fusion(f32[256,64,128]{0,2,1:T(8,128)S(1)} %copy-done.6, f32[256,1,128]{0,2,1:T(8,128)S(1)} %copy.82, f32[256,1,128]{0,2,1:T(8,128)S(1)} %copy.84, f32[256,66,1]{0,2,1:T(1,128)S(1)} %copy.90, f32[256,66,1]{0,2,1:T(1,128)S(1)} %copy.88, f32[64,128]{1,0:T(8,128)S(1)} %copy-done.8, ...), kind=kLoop, calls=%fused_computation.36 | loop fusion | flops 50331648 | bytes 13078528 | tf_op jit(solution)/shard_map/convert_element_type | solution.py:51
  155.8 74.1 %all-gather.3.cloned.1.call-done = f32[8192,256]{1,0:T(8,128)} async-done(((f32[256,256]{1,0:T(8,128)}), f32[8192,256]{1,0:T(8,128)}) %all-gather.3.cloned.1.call-update) | async-done | bytes 8388624 | tf_op jit(solution)/shard_map/all_gather | solution.py:53
  229.9 3.9 %reduce_sum.11 = f32[256,256]{1,0:T(8,128)S(1)} reduce(f32[32,256,256]{2,1,0:T(8,128)} %bitcast.48, f32[]{:T(128)} %constant.84.clone.1), dimensions={0}, to_apply=%region_0.0 | reduce | flops 2031616 | bytes 8650756 | tf_op jit(solution)/shard_map/reduce_sum | solution.py:53
  234.0 11.7 %cholesky.50 = f32[128,128]{1,0:T(8,128)S(1)} custom-call(f32[128,128]{1,0:T(8,128)S(1)} %cholesky.118), custom_call_target="Cholesky" | custom-call | tf_op jit(solution)/shard_map/jit(cholesky)/cholesky | solution.py:55
  245.8 9.8 %custom-call.14 = f32[1,128,128]{1,2,0:T(8,128)S(1)} custom-call(f32[1,128,128]{2,1,0:T(8,128)S(1)} %get-tuple-element.54), custom_call_target="InvertDiagBlocksLowerTriangular" | custom-call | tf_op jit(solution)/shard_map/jit(cholesky)/cholesky | solution.py:55
  256.1 11.7 %cholesky.105 = f32[128,128]{1,0:T(8,128)S(1)} custom-call(f32[128,128]{1,0:T(8,128)S(1)} %convolution_subtract_fusion.1), custom_call_target="Cholesky" | custom-call | tf_op jit(solution)/shard_map/jit(cholesky)/cholesky | solution.py:55
  270.2 4.1 %while.1 = (s32[]{:T(128)}, f32[256,256]{1,0:T(8,128)S(1)}, s32[2,2]{1,0:T(2,128)S(1)}, f32[2,128,128]{2,1,0:T(8,128)S(1)}, s32[]{:T(128)}) while((s32[]{:T(128)}, f32[256,256]{1,0:T(8,128)S(1)}, s32[2,2]{1,0:T(2,128)S(1)}, f32[2,128,128]{2,1,0:T(8,128)S(1)}, s32[]{:T(128)}) %tuple.41), condition=%wide.while_cond, body=%wide.while_body.sunk | while | flops 2 | bytes 131181 | solution.py:56
  274.3 19.7 %custom-call.15 = f32[2,128,128]{1,2,0:T(8,128)S(1)} custom-call(f32[2,128,128]{2,1,0:T(8,128)S(1)} %get-tuple-element.10), custom_call_target="InvertDiagBlocksLowerTriangular" | custom-call | tf_op jit(solution)/shard_map/triangular_solve | solution.py:56
  294.9 3.5 %fusion = bf16[32,8,64,128]{3,1,2,0:T(8,128)(2,1)S(1)} fusion(bf16[256,8192]{0,1:T(8,128)(2,1)} %bitcast.45, bf16[128,256]{1,0:T(8,128)(2,1)S(1)} %convolution_convert_fusion.1, bf16[128,256]{1,0:T(8,128)(2,1)S(1)} %get-tuple-element.57), kind=kOutput, calls=%fused_computation.40 | convolution fusion | flops 1076101120 | bytes 8519680 | tf_op jit(solution)/shard_map/dot_general | solution.py:59
  298.3 3.2 %copy.97 = bf16[32,8,64,128]{3,2,1,0:T(8,128)(2,1)} copy(bf16[32,8,64,128]{3,1,2,0:T(8,128)(2,1)S(1)} %fusion) | data formatting | bytes 8388608
  (115 shorter events, 50.6 us)
Async XLA Ops:
  7.2 222.7 %all-gather.3.cloned.1.call-start = ((), (), s32[]{:S(2)}) async-start(), calls=%async_computation | async-start | bytes 8650752 | tf_op jit(solution)/shard_map/all_gather | solution.py:53
  15.0 12.3 %collective-permute-start = (f32[256,1,128]{2,0,1:T(8,128)S(1)}, f32[256,1,128]{2,0,1:T(8,128)S(1)}, u32[]{:S(2)}, u32[]{:S(2)}) collective-permute-start(f32[256,1,128]{2,0,1:T(8,128)S(1)} %copy.51), channel_id=1, source_target_pairs={{2,0},{4,2},{6,4},{8,6},{10,8},{12,10},{14,12},{16,14},{18,16},{20... | collective-permute-start | bytes 393224 | tf_op jit(solution)/shard_map/ppermute | solution.py:18
  20.6 14.8 %copy-start.8 = (f32[64,128]{1,0:T(8,128)S(1)}, f32[64,128]{1,0:T(8,128)}, u32[]{:S(2)}) copy-start(f32[64,128]{1,0:T(8,128)} %param.7) | copy-start | bytes 98308
  20.6 14.8 %copy-start.9 = (f32[64,128]{1,0:T(8,128)S(1)}, f32[64,128]{1,0:T(8,128)}, u32[]{:S(2)}) copy-start(f32[64,128]{1,0:T(8,128)} %param.6) | copy-start | bytes 98308
  20.7 14.7 %copy-start.10 = (f32[64,128]{1,0:T(8,128)S(1)}, f32[64,128]{1,0:T(8,128)}, u32[]{:S(2)}) copy-start(f32[64,128]{1,0:T(8,128)} %param.5) | copy-start | bytes 98308
  20.7 7.1 %collective-permute-start.1 = (f32[256,1,128]{2,0,1:T(8,128)S(1)}, f32[256,1,128]{2,0,1:T(8,128)S(1)}, u32[]{:S(2)}, u32[]{:S(2)}) collective-permute-start(f32[256,1,128]{2,0,1:T(8,128)S(1)} %copy.53), channel_id=1, source_target_pairs={{0,2},{2,4},{4,6},{6,8},{8,10},{10,12},{12,14},{14,16},{16,18},{18... | collective-permute-start | bytes 393224 | tf_op jit(solution)/shard_map/ppermute | solution.py:15
  27.9 7.5 %copy-start.7 = (f32[256,64,128]{0,2,1:T(8,128)S(1)}, f32[256,64,128]{0,2,1:T(8,128)}, u32[]{:S(2)}) copy-start(f32[256,64,128]{0,2,1:T(8,128)} %convert_element_type.11) | copy-start | bytes 25165828
  29.4 4.4 %collective-permute-start.2 = (f32[256,66,1]{0,1,2:T(8,128)S(1)}, f32[256,66,1]{0,1,2:T(8,128)S(1)}, u32[]{:S(2)}, u32[]{:S(2)}) collective-permute-start(f32[256,66,1]{0,1,2:T(8,128)S(1)} %copy.57), channel_id=1, source_target_pairs={{1,0},{0,1},{3,2},{2,3},{5,4},{4,5},{7,6},{6,7},{9,8},{8,9},{11,10... | collective-permute-start | bytes 202760 | tf_op jit(solution)/shard_map/ppermute | solution.py:18
  30.9 4.4 %collective-permute-start.3 = (f32[256,66,1]{0,1,2:T(8,128)S(1)}, f32[256,66,1]{0,1,2:T(8,128)S(1)}, u32[]{:S(2)}, u32[]{:S(2)}) collective-permute-start(f32[256,66,1]{0,1,2:T(8,128)S(1)} %copy.59), channel_id=1, source_target_pairs={{0,1},{1,0},{2,3},{3,2},{4,5},{5,4},{6,7},{7,6},{8,9},{9,8},{10,11... | collective-permute-start | bytes 202760 | tf_op jit(solution)/shard_map/ppermute | solution.py:15
  53.7 5.2 %collective-permute-start.4 = (f32[256,1,128]{2,0,1:T(8,128)S(1)}, f32[256,1,128]{2,0,1:T(8,128)S(1)}, u32[]{:S(2)}, u32[]{:S(2)}) collective-permute-start(f32[256,1,128]{2,0,1:T(8,128)S(1)} %copy.61), channel_id=1, source_target_pairs={{2,0},{4,2},{6,4},{8,6},{10,8},{12,10},{14,12},{16,14},{18,16},{20... | collective-permute-start | bytes 393224 | tf_op jit(solution)/shard_map/ppermute | solution.py:18
  56.5 7.1 %collective-permute-start.5 = (f32[256,1,128]{2,0,1:T(8,128)S(1)}, f32[256,1,128]{2,0,1:T(8,128)S(1)}, u32[]{:S(2)}, u32[]{:S(2)}) collective-permute-start(f32[256,1,128]{2,0,1:T(8,128)S(1)} %copy.63), channel_id=1, source_target_pairs={{0,2},{2,4},{4,6},{6,8},{8,10},{10,12},{12,14},{14,16},{16,18},{18... | collective-permute-start | bytes 393224 | tf_op jit(solution)/shard_map/ppermute | solution.py:15
  63.8 7.0 %copy-start.2 = (f32[256,64,128]{0,2,1:T(8,128)S(1)}, f32[256,64,128]{0,2,1:T(8,128)}, u32[]{:S(2)}) copy-start(f32[256,64,128]{0,2,1:T(8,128)} %copy-done.1) | copy-start | bytes 25165828
  65.2 4.4 %collective-permute-start.6 = (f32[256,66,1]{0,1,2:T(8,128)S(1)}, f32[256,66,1]{0,1,2:T(8,128)S(1)}, u32[]{:S(2)}, u32[]{:S(2)}) collective-permute-start(f32[256,66,1]{0,1,2:T(8,128)S(1)} %copy.67), channel_id=1, source_target_pairs={{1,0},{0,1},{3,2},{2,3},{5,4},{4,5},{7,6},{6,7},{9,8},{8,9},{11,10... | collective-permute-start | bytes 202760 | tf_op jit(solution)/shard_map/ppermute | solution.py:18
  66.4 4.4 %collective-permute-start.7 = (f32[256,66,1]{0,1,2:T(8,128)S(1)}, f32[256,66,1]{0,1,2:T(8,128)S(1)}, u32[]{:S(2)}, u32[]{:S(2)}) collective-permute-start(f32[256,66,1]{0,1,2:T(8,128)S(1)} %copy.69), channel_id=1, source_target_pairs={{0,1},{1,0},{2,3},{3,2},{4,5},{5,4},{6,7},{7,6},{8,9},{9,8},{10,11... | collective-permute-start | bytes 202760 | tf_op jit(solution)/shard_map/ppermute | solution.py:15
  89.1 2.6 collective-permute-start.8
  89.3 7.1 %collective-permute-start.9 = (f32[256,1,128]{2,0,1:T(8,128)S(1)}, f32[256,1,128]{2,0,1:T(8,128)S(1)}, u32[]{:S(2)}, u32[]{:S(2)}) collective-permute-start(f32[256,1,128]{2,0,1:T(8,128)S(1)} %copy.73), channel_id=1, source_target_pairs={{0,2},{2,4},{4,6},{6,8},{8,10},{10,12},{12,14},{14,16},{16,18},{18... | collective-permute-start | bytes 393224 | tf_op jit(solution)/shard_map/ppermute | solution.py:15
  96.6 6.9 %copy-start.4 = (f32[256,64,128]{0,2,1:T(8,128)S(1)}, f32[256,64,128]{0,2,1:T(8,128)}, u32[]{:S(2)}) copy-start(f32[256,64,128]{0,2,1:T(8,128)} %copy-done.3) | copy-start | bytes 25165828
  98.0 4.4 %collective-permute-start.10 = (f32[256,66,1]{0,1,2:T(8,128)S(1)}, f32[256,66,1]{0,1,2:T(8,128)S(1)}, u32[]{:S(2)}, u32[]{:S(2)}) collective-permute-start(f32[256,66,1]{0,1,2:T(8,128)S(1)} %copy.77), channel_id=1, source_target_pairs={{1,0},{0,1},{3,2},{2,3},{5,4},{4,5},{7,6},{6,7},{9,8},{8,9},{11,10... | collective-permute-start | bytes 202760 | tf_op jit(solution)/shard_map/ppermute | solution.py:18
  99.1 4.4 %collective-permute-start.11 = (f32[256,66,1]{0,1,2:T(8,128)S(1)}, f32[256,66,1]{0,1,2:T(8,128)S(1)}, u32[]{:S(2)}, u32[]{:S(2)}) collective-permute-start(f32[256,66,1]{0,1,2:T(8,128)S(1)} %copy.79), channel_id=1, source_target_pairs={{0,1},{1,0},{2,3},{3,2},{4,5},{5,4},{6,7},{7,6},{8,9},{9,8},{10,11... | collective-permute-start | bytes 202760 | tf_op jit(solution)/shard_map/ppermute | solution.py:15
  121.8 2.6 collective-permute-start.12
  122.0 7.1 %collective-permute-start.13 = (f32[256,1,128]{2,0,1:T(8,128)S(1)}, f32[256,1,128]{2,0,1:T(8,128)S(1)}, u32[]{:S(2)}, u32[]{:S(2)}) collective-permute-start(f32[256,1,128]{2,0,1:T(8,128)S(1)} %copy.83), channel_id=1, source_target_pairs={{0,2},{2,4},{4,6},{6,8},{8,10},{10,12},{12,14},{14,16},{16,18},{18... | collective-permute-start | bytes 393224 | tf_op jit(solution)/shard_map/ppermute | solution.py:15
  129.2 7.0 %copy-start.6 = (f32[256,64,128]{0,2,1:T(8,128)S(1)}, f32[256,64,128]{0,2,1:T(8,128)}, u32[]{:S(2)}) copy-start(f32[256,64,128]{0,2,1:T(8,128)} %copy-done.5) | copy-start | bytes 25165828
  130.7 4.4 %collective-permute-start.14 = (f32[256,66,1]{0,1,2:T(8,128)S(1)}, f32[256,66,1]{0,1,2:T(8,128)S(1)}, u32[]{:S(2)}, u32[]{:S(2)}) collective-permute-start(f32[256,66,1]{0,1,2:T(8,128)S(1)} %copy.87), channel_id=1, source_target_pairs={{1,0},{0,1},{3,2},{2,3},{5,4},{4,5},{7,6},{6,7},{9,8},{8,9},{11,10... | collective-permute-start | bytes 202760 | tf_op jit(solution)/shard_map/ppermute | solution.py:18
  131.8 4.4 %collective-permute-start.15 = (f32[256,66,1]{0,1,2:T(8,128)S(1)}, f32[256,66,1]{0,1,2:T(8,128)S(1)}, u32[]{:S(2)}, u32[]{:S(2)}) collective-permute-start(f32[256,66,1]{0,1,2:T(8,128)S(1)} %copy.89), channel_id=1, source_target_pairs={{0,1},{1,0},{2,3},{3,2},{4,5},{5,4},{6,7},{7,6},{8,9},{9,8},{10,11... | collective-permute-start | bytes 202760 | tf_op jit(solution)/shard_map/ppermute | solution.py:15
  (4 other events, 11.8 us)
Sparse Core Ops, SparseCore 0:
  155.8 73.9 all-gather.2
